TPU v7x, 128 devices: a whole 4x4x4 slice. The times are simulated.
128 devices in a mesh: row: 32 (over y, x, core), col: 4 (over z).
Axes of the slice: x: 4, y: 4, z: 4, core: 2. Of those that a mesh axis runs over, the one named last changes fastest.
Arguments:
- embeddings: float32 [16384, 256], P(('col', 'row')), may hold values from -6 to 6
- levels: int32 [16384], P('row'), may hold values from 0 to 7
Outputs:
- responsibility: float32 [16384, 16384], P('row', 'col')
- availability: float32 [16384, 16384], P('row', 'col')
All inputs are finite; a program needn't handle non-finite values.
Results may differ from a plain program's by a relative error of at most 0.0003.
Values sent between devices are 32-bit elements; how exact they have to be, the bound alone decides.
No kernel may reach another device: no remote copies, remote signals or barrier semaphores. Data moves between devices by JAX's collectives and lax.ppermute only.
A program may use at most 64 MiB of HBM per device.

v0:
```python
import jax
import jax.numpy as jnp
from jax import lax
from jax.sharding import PartitionSpec as P

ITERS = 2
lowest_value = -1e30


def broadcast(shard, axis, root):
    return lax.dynamic_index_in_dim(lax.all_gather(shard, axis), root, 0, keepdims=False)


def rows_first(arrays, axis, dims):
    turned = [jnp.moveaxis(a, dim, 0) for a, dim in zip(arrays, dims)]
    both = jnp.concatenate([t.reshape(len(t), -1) for t in turned], axis=1)
    out, at, finished = (lax.all_gather(both, axis, axis=0, tiled=True), 0, [])
    for t, dim in zip(turned, dims):
        share = out[:, at : at + t[0].size].reshape(-1, *t.shape[1:])
        finished.append(jnp.moveaxis(share, 0, dim))
        at += t[0].size
    return tuple(finished)


def copy_for_each(shard, axis):
    copies = jnp.broadcast_to(shard, (lax.axis_size(axis), *shard.shape))
    return lax.all_to_all(copies, axis, split_axis=0, concat_axis=0, tiled=True)


def over_copies(shard, axis):
    return copy_for_each(shard, axis).sum(axis=0)


def packed_total(arrays, axis):
    vector, at, finished = (jnp.concatenate([a.reshape(-1) for a in arrays]), 0, [])
    subtotal = over_copies(vector, axis)
    for a in arrays:
        finished.append(subtotal[at : at + a.size].reshape(a.shape))
        at += a.size
    return tuple(finished)


def normalize(vectors):
    return vectors * lax.rsqrt(jnp.sum(vectors * vectors, axis=1, keepdims=True) + 1e-06)


def top_two(values):
    best_value = jnp.max(values, axis=1, keepdims=True)
    tie_count = jnp.sum(jnp.where(values == best_value, 1, 0), axis=1, keepdims=True)
    remainder = jnp.max(jnp.where(values < best_value, values, lowest_value), axis=1, keepdims=True)
    return (best_value, jnp.where(tie_count > 1, best_value, remainder))


def shards(embeddings, levels):
    row_count = levels.shape[0]
    n_row = lax.axis_size("row")
    n_col = lax.axis_size("col")
    row_idx = lax.axis_index("row")
    col_idx = lax.axis_index("col")
    span_rows = embeddings.shape[0]
    col_count = span_rows * n_row
    preference = 0.25 * levels.astype(jnp.float32) - 1.0
    column_block = lax.all_gather(embeddings, "row", axis=0, tiled=True)
    group_size = n_row // n_col
    offset = row_idx % group_size * row_count
    row_piece = lax.dynamic_slice_in_dim(column_block, offset, row_count, 0)
    row_block = broadcast(row_piece, "col", row_idx // group_size)
    unit_rows = normalize(row_block)
    unit_cols = normalize(column_block)
    product = lax.dot_general(
        unit_rows,
        unit_cols,
        (((1,), (1,)), ((), ())),
        precision=lax.Precision.HIGHEST,
        preferred_element_type=jnp.float32,
    )
    global_rows = row_idx * row_count + jnp.arange(row_count, dtype=jnp.int32)
    global_cols = col_idx * col_count + jnp.arange(col_count, dtype=jnp.int32)
    diagonal_mask = global_rows[:, None] == global_cols[None, :]
    similar = jnp.where(diagonal_mask, preference[:, None], product)
    responsibility = jnp.zeros_like(similar)
    availability = jnp.zeros_like(similar)
    for iteration in range(ITERS):
        combined = availability + similar
        best_value, second_value = top_two(combined)
        gathered_best, gathered_second = rows_first((best_value, second_value), "col", (1, 1))
        best_value, runner_up = top_two(gathered_best)
        second_value = jnp.maximum(runner_up, jnp.max(gathered_second, axis=1, keepdims=True))
        fresh = similar - jnp.where(combined >= best_value, second_value, best_value)
        responsibility = 0.5 * responsibility + 0.5 * fresh
        positive = jnp.sum(jnp.where(diagonal_mask, 0.0, jnp.maximum(responsibility, 0.0)), axis=0)
        diag_part = jnp.sum(jnp.where(diagonal_mask, responsibility, 0.0), axis=0)
        column_positive, self_resp = packed_total((positive, diag_part), "row")
        renewed = jnp.where(
            diagonal_mask,
            column_positive[None, :],
            jnp.minimum(
                0.0,
                self_resp[None, :] + column_positive[None, :] - jnp.maximum(responsibility, 0.0),
            ),
        )
        availability = 0.5 * availability + 0.5 * renewed
    return (responsibility, availability)


def solution(mesh):
    placed = (P(("col", "row"), None), P("row"))
    return jax.shard_map(
        shards,
        mesh=mesh,
        in_specs=placed,
        out_specs=(P("row", "col"), P("row", "col")),
        check_vma=False,
    )
```

profile of v0, /device:TPU:1, one launch (start us, length us, event | category | flops | bytes accessed | tf_op | source)
XLA Modules:
  0.0 213.9 jit_solution(4717225558266819181)
XLA Ops:
  7.2 0.0 all-gather.6.cloned.1.call-start
  7.2 0.7 all-gather.6.cloned.1.call-update
  7.9 0.0 all-gather.8.cloned.1.call-start
  8.0 51.8 %all-gather.6.cloned.1.call-done = f32[4096,256]{1,0:T(8,128)} async-done(((f32[128,256]{1,0:T(8,128)}), f32[4096,256]{1,0:T(8,128)}) %all-gather.6.cloned.1.call-update) | async-done | bytes 4194320 | tf_op jit(solution)/shard_map/all_gather | solution.py:63
  59.8 1.9 constant_dynamic-slice_fusion
  61.6 0.0 all-gather.8.cloned.1.call-update
  61.7 0.7 multiply_add_fusion.2
  62.4 2.8 %multiply_reduce_fusion = f32[4096]{0:T(1024)S(1)} fusion(f32[4096,256]{1,0:T(8,128)} %all-gather.6.cloned.1.call-done), kind=kLoop, calls=%fused_computation.24 | loop fusion | flops 2093056 | bytes 4210688 | tf_op jit(solution)/shard_map/reduce_sum | solution.py:44
  65.2 26.7 %all-gather.8.cloned.1.call-done = f32[2048,256]{1,0:T(8,128)} async-done(((f32[512,256]{1,0:T(8,128)}), f32[2048,256]{1,0:T(8,128)}) %all-gather.8.cloned.1.call-update) | async-done | bytes 2097168 | tf_op jit(solution)/shard_map/all_gather | solution.py:11
  91.9 1.2 fusion.11
  93.1 10.4 %fusion.20 = (f32[512]{0:T(512)S(1)}, f32[512,4096]{1,0:T(8,128)S(1)}) fusion(f32[4096,256]{1,0:T(8,128)} %all-gather.6.cloned.1.call-done, f32[4096]{0:T(1024)S(1)} %add_rsqrt_fusion, f32[4,512,256]{2,1,0:T(8,128)} %bitcast.36, s32[]{:T(128)S(6)} %select_n.121, f32[512]{0:T(512)S(1)} %add_rsqrt_fusion.1, f32[512]{0:T(512)S(1)} %multiply_add_fusion.2, ...), kind=kOutput, calls=%fused_computation.67 | convolution fusion | flops 6449921536 | bytes 13148164 | tf_op jit(solution)/shard_map/dot_general | solution.py:70
  103.5 0.0 copy-start
  103.5 1.0 fusion.6
  104.4 1.0 select_reduce_fusion.1
  105.5 9.1 %all-gather.1 = f32[4,1,1024]{2,1,0:T(1,128)S(1)} all-gather(f32[1,1,1024]{2,1,0:T(1,128)S(1)} %maximum_bitcast_fusion), channel_id=1, replica_groups=mesh['row'=32,'col'=4] {'col'}, dimensions={0}, use_global_device_ids=true | all-gather | bytes 20480 | tf_op jit(solution)/shard_map/all_gather | solution.py:17
  114.7 0.0 copy-done
  114.7 3.5 %fusion = (f32[4096]{0:T(1024)S(1)}, f32[4096]{0:T(1024)S(1)}) fusion(f32[512,4096]{1,0:T(8,128)S(1)} %get-tuple-element.18, f32[512]{0:T(512)S(1)} %select_maximum_fusion.1, f32[512]{0:T(512)S(1)} %get-tuple-element.8, s32[4096]{0:T(1024)S(1)} %iota_add_fusion, s32[512]{0:T(512)S(1)} %iota_add_fusion.1), kind=kLoop, calls=%fused_computation.9 | loop fusion | flops 20963328 | bytes 8443904 | tf_op jit(solution)/shard_map/reduce_sum | solution.py:91
  118.2 0.9 broadcast_in_dim.120
  119.2 27.4 %all_to_all.12 = f32[32,1,8192]{2,1,0:T(1,128)S(1)} all-to-all(f32[32,1,8192]{2,1,0:T(1,128)S(1)} %broadcast_in_dim.120), channel_id=1, replica_groups=mesh['row'=32,'col'=4] {'row'}, dimensions={0} | all-to-all | bytes 2097152 | tf_op jit(solution)/shard_map/all_to_all | solution.py:27
  146.6 0.7 reduce_sum.114
  147.3 6.0 %fusion.17 = (f32[512]{0:T(512)S(1)}, f32[512,4096]{1,0:T(8,128)S(1)}) fusion(f32[512,4096]{1,0:T(8,128)} %copy-done, f32[512]{0:T(512)S(1)} %select_maximum_fusion.1, f32[512]{0:T(512)S(1)} %get-tuple-element.8, f32[4096]{0:T(1024)S(1)} %get-tuple-element.16, f32[4096]{0:T(1024)S(1)} %get-tuple-element.15, s32[4096]{0:T(1024)S(1)} %iota_add_fusion, ...), kind=kLoop, calls=%fused_computation.64 | loop fusion | flops 25165312 | bytes 16834560 | tf_op jit(solution)/shard_map/reduce_max | solution.py:48
  153.4 0.0 slice-start
  153.4 1.0 fusion.7
  154.3 0.0 slice-start.1
  154.4 1.0 select_reduce_fusion
  155.4 9.3 %all-gather.2 = f32[4,1,1024]{2,1,0:T(1,128)S(1)} all-gather(f32[1,1,1024]{2,1,0:T(1,128)S(1)} %maximum_bitcast_fusion.1), channel_id=1, replica_groups=mesh['row'=32,'col'=4] {'col'}, dimensions={0}, use_global_device_ids=true | all-gather | bytes 20480 | tf_op jit(solution)/shard_map/all_gather | solution.py:17
  164.8 0.0 slice-done
  164.8 0.0 slice-done.1
  164.8 6.7 %fusion.2 = (f32[4096]{0:T(1024)S(1)}, f32[4096]{0:T(1024)S(1)}, f32[512,4096]{1,0:T(8,128)}) fusion(s32[4096]{0:T(1024)S(1)} %iota_add_fusion, s32[512]{0:T(512)S(1)} %iota_add_fusion.1, f32[512,4096]{1,0:T(8,128)S(1)} %bitcast.34, f32[512]{0:T(512)S(1)} %select_maximum_fusion, f32[512,4096]{1,0:T(8,128)S(1)} %get-tuple-element.12, ...), kind=kLoop, calls=%fused_computation.11 | loop fusion | flops 31449088 | bytes 25225216 | tf_op jit(solution)/shard_map/reduce_sum | solution.py:91
  171.5 0.9 broadcast_in_dim.123
  172.4 23.3 %all_to_all.13 = f32[32,1,8192]{2,1,0:T(1,128)S(1)} all-to-all(f32[32,1,8192]{2,1,0:T(1,128)S(1)} %broadcast_in_dim.123), channel_id=1, replica_groups=mesh['row'=32,'col'=4] {'row'}, dimensions={0} | all-to-all | bytes 2097152 | tf_op jit(solution)/shard_map/all_to_all | solution.py:27
  195.7 0.7 reduce_sum.119
  196.4 10.6 %fusion.5 = f32[512,4096]{1,0:T(8,128)} fusion(f32[512,4096]{1,0:T(8,128)} %get-tuple-element.10, f32[512,4096]{1,0:T(8,128)} %copy-done, f32[4096]{0:T(1024)S(1)} %get-tuple-element.14, f32[4096]{0:T(1024)S(1)} %get-tuple-element.13, f32[4096]{0:T(1024)S(1)} %get-tuple-element.16, f32[4096]{0:T(1024)S(1)} %get-tuple-element.15, ...), kind=kLoop, calls=%fused_computation.14 | loop fusion | flops 33554432 | bytes 25253888 | tf_op jit(solution)/shard_map/add | solution.py:102
  (25 shorter events, 0.2 us)
Async XLA Ops:
  7.2 52.6 %all-gather.6.cloned.1.call-start = ((), (), s32[]{:S(2)}) async-start(), calls=%async_computation.2 | async-start | bytes 4325376 | tf_op jit(solution)/shard_map/all_gather | solution.py:63
  7.9 84.0 %all-gather.8.cloned.1.call-start = ((), (), s32[]{:S(2)}) async-start(), calls=%async_computation.3 | async-start | bytes 2621440 | tf_op jit(solution)/shard_map/all_gather | solution.py:11
  103.5 11.3 %copy-start = (f32[512,4096]{1,0:T(8,128)}, f32[512,4096]{1,0:T(8,128)S(1)}, u32[]{:S(2)}) copy-start(f32[512,4096]{1,0:T(8,128)S(1)} %get-tuple-element.18) | copy-start | bytes 25165828
  153.4 11.4 %slice-start = ((s8[8388608]{0:T(1024)(128)(4,1)}), s8[4194304]{0:T(1024)(128)(4,1)S(1)}, s32[]{:S(2)}) async-start(s8[8388608]{0:T(1024)(128)(4,1)} %bitcast.33), calls=%async_computation.4 | async-start | bytes 8388608
  154.3 10.4 %slice-start.1 = ((s8[8388608]{0:T(1024)(128)(4,1)}), s8[4194304]{0:T(1024)(128)(4,1)S(1)}, s32[]{:S(2)}) async-start(s8[8388608]{0:T(1024)(128)(4,1)} %bitcast.33), calls=%async_computation.5 | async-start | bytes 8388608
Sparse Core Ops, SparseCore 0:
  10.2 49.4 all-gather.5
  62.0 29.8 all-gather.7
where the time goes:
time: 214 us
  waiting for transfers between devices  79.2 us (37%)
  blocking collectives  69.1 us (32%)
  other arithmetic  37.1 us (17%)
  between operations  14.3 us (7%)
  matrix products  10.4 us (5%)
  local copies, waits for them, and re-layouts  3.76 us (2%)
    all_gather x1, waiting for transfers between devices, shards(): column_block = lax.all_gather(embeddings, 'row', axis=0, tiled=True)  51.8 us
    all_to_all x2, blocking collectives, copy_for_each(): return lax.all_to_all(copies, axis, split_axis=0, concat_axis=0, tiled=True)  50.7 us
    all_gather x1, waiting for transfers between devices, broadcast(): lax.all_gather(shard, axis)  26.7 us
    all_gather x2, blocking collectives, rows_first(): out, at, finished = (lax.all_gather(both, axis, axis=0, tiled=True), 0, [])  18.4 us
    add x1, other arithmetic, shards(): availability = 0.5 * availability + 0.5 * renewed  10.6 us
    dot_general x1, matrix products, shards(): lax.dot_general(unit_rows, unit_cols, (((1,), (1,)), ((), ())), precision...  10.4 us
    reduce_sum x2, other arithmetic, shards(): jnp.sum(jnp.where(diagonal_mask, 0.0, jnp.maximum(responsibility, 0.0)),...  10.2 us
    reduce_max x3, other arithmetic, top_two(): best_value = jnp.max(values, axis=1, keepdims=True)  6.09 us
  transfers between devices with their start and end apart: 2, of which 2 were waited for; matrix products, arithmetic and copies ran while one was open for 2% of the time, Pallas kernels for 0%

commit v1 on v0

--- a/solution.py
+++ b/solution.py
@@ -2,6 +2,7 @@
 import jax.numpy as jnp
 from jax import lax
 from jax.sharding import PartitionSpec as P
+from jax.lax import all_to_all, axis_size
 
 ITERS = 2
 lowest_value = -1e30
@@ -14,7 +15,13 @@
 def rows_first(arrays, axis, dims):
     turned = [jnp.moveaxis(a, dim, 0) for a, dim in zip(arrays, dims)]
     both = jnp.concatenate([t.reshape(len(t), -1) for t in turned], axis=1)
-    out, at, finished = (lax.all_gather(both, axis, axis=0, tiled=True), 0, [])
+    out, at, finished = (
+        jnp.concatenate(
+            all_to_all(jnp.stack([both for _ in range(axis_size(axis))], 0), axis, 0, 0), 0
+        ),
+        0,
+        [],
+    )
     for t, dim in zip(turned, dims):
         share = out[:, at : at + t[0].size].reshape(-1, *t.shape[1:])
         finished.append(jnp.moveaxis(share, 0, dim))

time: 214 us -> 206 us (0.963)
  blocking collectives: 69.1 us -> 61 us
    all_gather x2 -> x0, blocking collectives: 18.4 us -> none  [rows_first(): out, at, finished = (lax.all_gather(both, axis, axis=0, tiled=True), 0, [])]
    all_to_all x0 -> x2, blocking collectives: none -> 13.4 us  [rows_first(): all_to_all(jnp.stack([both for _ in range(axis_size(axis))], 0), axis, 0, 0)]
    all_to_all x2, blocking collectives: 50.7 us -> 47.5 us  [copy_for_each(): return lax.all_to_all(copies, axis, split_axis=0, concat_axis=0, tiled=True)]
where the time goes in v1:
time: 206 us
  waiting for transfers between devices  79.2 us (38%)
  blocking collectives  61 us (30%)
  other arithmetic  37.1 us (18%)
  between operations  14.3 us (7%)
  matrix products  10.4 us (5%)
  local copies, waits for them, and re-layouts  3.78 us (2%)
    all_gather x1, waiting for transfers between devices, shards(): column_block = lax.all_gather(embeddings, 'row', axis=0, tiled=True)  51.8 us
    all_to_all x2, blocking collectives, copy_for_each(): return lax.all_to_all(copies, axis, split_axis=0, concat_axis=0, tiled=True)  47.5 us
    all_gather x1, waiting for transfers between devices, broadcast(): lax.all_gather(shard, axis)  26.7 us
    all_to_all x2, blocking collectives, rows_first(): all_to_all(jnp.stack([both for _ in range(axis_size(axis))], 0), axis, 0, 0)  13.4 us
    add x1, other arithmetic, shards(): availability = 0.5 * availability + 0.5 * renewed  10.6 us
    dot_general x1, matrix products, shards(): lax.dot_general(unit_rows, unit_cols, (((1,), (1,)), ((), ())), precision...  10.4 us
    reduce_sum x2, other arithmetic, shards(): jnp.sum(jnp.where(diagonal_mask, 0.0, jnp.maximum(responsibility, 0.0)),...  10.2 us
    reduce_max x3, other arithmetic, top_two(): best_value = jnp.max(values, axis=1, keepdims=True)  6.09 us
  transfers between devices with their start and end apart: 2, of which 2 were waited for; matrix products, arithmetic and copies ran while one was open for 2% of the time, Pallas kernels for 0%

profile of v1, /device:TPU:1, one launch (start us, length us, event | category | flops | bytes accessed | tf_op | source)
XLA Modules:
  0.0 205.8 jit_solution(14031393907567653832)
XLA Ops:
  7.2 0.0 all-gather.4.cloned.1.call-start
  7.2 0.7 all-gather.4.cloned.1.call-update
  7.9 0.0 all-gather.6.cloned.1.call-start
  8.0 51.8 %all-gather.4.cloned.1.call-done = f32[4096,256]{1,0:T(8,128)} async-done(((f32[128,256]{1,0:T(8,128)}), f32[4096,256]{1,0:T(8,128)}) %all-gather.4.cloned.1.call-update) | async-done | bytes 4194320 | tf_op jit(solution)/shard_map/all_gather | solution.py:70
  59.8 1.9 constant_dynamic-slice_fusion
  61.6 0.0 all-gather.6.cloned.1.call-update
  61.7 0.7 multiply_add_fusion.2
  62.4 2.8 %multiply_reduce_fusion = f32[4096]{0:T(1024)S(1)} fusion(f32[4096,256]{1,0:T(8,128)} %all-gather.4.cloned.1.call-done), kind=kLoop, calls=%fused_computation.24 | loop fusion | flops 2093056 | bytes 4210688 | tf_op jit(solution)/shard_map/reduce_sum | solution.py:51
  65.2 26.7 %all-gather.6.cloned.1.call-done = f32[2048,256]{1,0:T(8,128)} async-done(((f32[512,256]{1,0:T(8,128)}), f32[2048,256]{1,0:T(8,128)}) %all-gather.6.cloned.1.call-update) | async-done | bytes 2097168 | tf_op jit(solution)/shard_map/all_gather | solution.py:12
  91.9 1.2 fusion.11
  93.1 10.4 %fusion.20 = (f32[512]{0:T(512)S(1)}, f32[512,4096]{1,0:T(8,128)S(1)}) fusion(f32[4096,256]{1,0:T(8,128)} %all-gather.4.cloned.1.call-done, f32[4096]{0:T(1024)S(1)} %add_rsqrt_fusion, f32[4,512,256]{2,1,0:T(8,128)} %bitcast.34, s32[]{:T(128)S(6)} %select_n.121, f32[512]{0:T(512)S(1)} %add_rsqrt_fusion.1, f32[512]{0:T(512)S(1)} %multiply_add_fusion.2, ...), kind=kOutput, calls=%fused_computation.67 | convolution fusion | flops 6449921536 | bytes 13148164 | tf_op jit(solution)/shard_map/dot_general | solution.py:77
  103.5 0.0 copy-start
  103.5 1.0 fusion.6
  104.4 1.0 select_reduce_fusion.1
  105.5 6.8 %all_to_all.22 = f32[4,1,1024]{2,1,0:T(1,128)S(1)} all-to-all(f32[4,1,1024]{2,1,0:T(1,128)S(1)} %stack.4), channel_id=1, replica_groups=mesh['row'=32,'col'=4] {'col'}, dimensions={0} | all-to-all | bytes 32768 | tf_op jit(solution)/shard_map/all_to_all | solution.py:20
  112.4 0.0 copy-done
  112.4 3.5 %fusion = (f32[4096]{0:T(1024)S(1)}, f32[4096]{0:T(1024)S(1)}) fusion(f32[512,4096]{1,0:T(8,128)S(1)} %get-tuple-element.18, f32[512]{0:T(512)S(1)} %select_maximum_fusion.1, f32[512]{0:T(512)S(1)} %get-tuple-element.8, s32[4096]{0:T(1024)S(1)} %iota_add_fusion, s32[512]{0:T(512)S(1)} %iota_add_fusion.1), kind=kLoop, calls=%fused_computation.9 | loop fusion | flops 20963328 | bytes 8443904 | tf_op jit(solution)/shard_map/reduce_sum | solution.py:98
  115.9 0.9 broadcast_in_dim.120
  116.8 26.0 %all_to_all.23 = f32[32,1,8192]{2,1,0:T(1,128)S(1)} all-to-all(f32[32,1,8192]{2,1,0:T(1,128)S(1)} %broadcast_in_dim.120), channel_id=1, replica_groups=mesh['row'=32,'col'=4] {'row'}, dimensions={0} | all-to-all | bytes 2097152 | tf_op jit(solution)/shard_map/all_to_all | solution.py:34
  142.8 0.7 reduce_sum.114
  143.5 6.0 %fusion.17 = (f32[512]{0:T(512)S(1)}, f32[512,4096]{1,0:T(8,128)S(1)}) fusion(f32[512,4096]{1,0:T(8,128)} %copy-done, f32[512]{0:T(512)S(1)} %select_maximum_fusion.1, f32[512]{0:T(512)S(1)} %get-tuple-element.8, f32[4096]{0:T(1024)S(1)} %get-tuple-element.16, f32[4096]{0:T(1024)S(1)} %get-tuple-element.15, s32[4096]{0:T(1024)S(1)} %iota_add_fusion, ...), kind=kLoop, calls=%fused_computation.64 | loop fusion | flops 25165312 | bytes 16834560 | tf_op jit(solution)/shard_map/reduce_max | solution.py:55
  149.6 0.0 slice-start
  149.6 1.0 fusion.7
  150.5 0.0 slice-start.1
  150.5 1.0 select_reduce_fusion
  151.6 6.7 %all_to_all.24 = f32[4,1,1024]{2,1,0:T(1,128)S(1)} all-to-all(f32[4,1,1024]{2,1,0:T(1,128)S(1)} %stack.5), channel_id=1, replica_groups=mesh['row'=32,'col'=4] {'col'}, dimensions={0} | all-to-all | bytes 32768 | tf_op jit(solution)/shard_map/all_to_all | solution.py:20
  158.4 0.0 slice-done
  158.4 0.0 slice-done.1
  158.4 6.7 %fusion.2 = (f32[4096]{0:T(1024)S(1)}, f32[4096]{0:T(1024)S(1)}, f32[512,4096]{1,0:T(8,128)}) fusion(s32[4096]{0:T(1024)S(1)} %iota_add_fusion, s32[512]{0:T(512)S(1)} %iota_add_fusion.1, f32[512,4096]{1,0:T(8,128)S(1)} %bitcast.32, f32[512]{0:T(512)S(1)} %select_maximum_fusion, f32[512,4096]{1,0:T(8,128)S(1)} %get-tuple-element.12, ...), kind=kLoop, calls=%fused_computation.11 | loop fusion | flops 31449088 | bytes 25225216 | tf_op jit(solution)/shard_map/reduce_sum | solution.py:98
  165.1 0.9 broadcast_in_dim.123
  166.1 21.5 %all_to_all.25 = f32[32,1,8192]{2,1,0:T(1,128)S(1)} all-to-all(f32[32,1,8192]{2,1,0:T(1,128)S(1)} %broadcast_in_dim.123), channel_id=1, replica_groups=mesh['row'=32,'col'=4] {'row'}, dimensions={0} | all-to-all | bytes 2097152 | tf_op jit(solution)/shard_map/all_to_all | solution.py:34
  187.6 0.7 reduce_sum.119
  188.3 10.6 %fusion.5 = f32[512,4096]{1,0:T(8,128)} fusion(f32[512,4096]{1,0:T(8,128)} %get-tuple-element.10, f32[512,4096]{1,0:T(8,128)} %copy-done, f32[4096]{0:T(1024)S(1)} %get-tuple-element.14, f32[4096]{0:T(1024)S(1)} %get-tuple-element.13, f32[4096]{0:T(1024)S(1)} %get-tuple-element.16, f32[4096]{0:T(1024)S(1)} %get-tuple-element.15, ...), kind=kLoop, calls=%fused_computation.14 | loop fusion | flops 33554432 | bytes 25253888 | tf_op jit(solution)/shard_map/add | solution.py:109
  (27 shorter events, 0.3 us)
Async XLA Ops:
  7.2 52.6 %all-gather.4.cloned.1.call-start = ((), (), s32[]{:S(2)}) async-start(), calls=%async_computation.4 | async-start | bytes 4325376 | tf_op jit(solution)/shard_map/all_gather | solution.py:70
  7.9 84.0 %all-gather.6.cloned.1.call-start = ((), (), s32[]{:S(2)}) async-start(), calls=%async_computation.5 | async-start | bytes 2621440 | tf_op jit(solution)/shard_map/all_gather | solution.py:12
  103.5 8.9 %copy-start = (f32[512,4096]{1,0:T(8,128)}, f32[512,4096]{1,0:T(8,128)S(1)}, u32[]{:S(2)}) copy-start(f32[512,4096]{1,0:T(8,128)S(1)} %get-tuple-element.18) | copy-start | bytes 25165828
  149.6 8.9 %slice-start = ((s8[8388608]{0:T(1024)(128)(4,1)}), s8[4194304]{0:T(1024)(128)(4,1)S(1)}, s32[]{:S(2)}) async-start(s8[8388608]{0:T(1024)(128)(4,1)} %bitcast.31), calls=%async_computation.6 | async-start | bytes 8388608
  150.5 7.9 %slice-start.1 = ((s8[8388608]{0:T(1024)(128)(4,1)}), s8[4194304]{0:T(1024)(128)(4,1)S(1)}, s32[]{:S(2)}) async-start(s8[8388608]{0:T(1024)(128)(4,1)} %bitcast.31), calls=%async_computation.7 | async-start | bytes 8388608
Sparse Core Ops, SparseCore 0:
  10.2 49.4 all-gather.3
  62.0 29.8 all-gather.5
